TPU v7x, 32 devices: a whole 2x2x4 slice. The times are simulated.
32 devices in a mesh: groups: 1, seq: 32 (over z, y, x, core).
Axes of the slice: x: 2, y: 2, z: 4, core: 2. Of those that a mesh axis runs over, the one named last changes fastest.
Arguments:
- video_heads: bfloat16 [16, 4, 1024, 384], P('groups', None, 'seq'), may hold values from -60 to 60
- image_heads: bfloat16 [16, 4, 512, 256], P('groups', None, 'seq'), may hold values from -6 to 6
- audio_queries: bfloat16 [2, 1024, 2048], P('groups', 'seq'), may hold values from -60 to 60
- audio_keys: bfloat16 [64, 4096], P('seq', 'groups'), may hold values from -8 to 8
- condition_flags: int32 [2, 4], P('groups'), may hold values from 0 to 1, as said below
- guidance_weights: int32 [4], P('groups'), may hold values from -8 to 24
- token_frame: int32 [1024], P('groups'), may hold values from 0 to 15, never falling along the last dimension, each value on 1 to 128 neighbouring positions
- window_start: int32 [16], P('groups'), may hold values from 0 to 32
- modulation: float32 [2, 4, 2048], P('groups'), may hold values from -3 to 3
- final_weight: bfloat16 [2048, 64], replicated, may hold values from -0.125 to 0.125
- noisy_latent: float32 [1024, 64], P(('groups', 'seq')), may hold values from -6 to 6
Outputs:
- velocity: float32 [1024, 64], P(('groups', 'seq'))
- next_latent: float32 [1024, 64], P(('groups', 'seq'))
Inputs may be any that keep to these rules, and one draw needn't show every extreme that they name: `condition_flags`: each of the four pairs (audio flag, image flag) occurs in exactly one branch.
All inputs are finite; a program needn't handle non-finite values.
Results may differ from a plain program's by a relative error of at most 0.0045.
Values may be sent and summed in bfloat16 or wider, within the bound.
A program may use at most 64 MiB of HBM per device.

v0:
```python
import functools
import math

import jax
import jax.numpy as jnp
from jax import lax
from jax.experimental import pallas as pl
from jax.experimental.pallas import tpu as pltpu
from jax.sharding import PartitionSpec as P

AUD_WIN = 32
PAIRS = ((1, 1), (1, 0), (0, 1), (0, 0))


def step_kernel(
    n,
    q_block,
    plane,
    flags_in,
    guide_in,
    frames_in,
    starts_in,
    video_in,
    image_in,
    audio_q_in,
    audio_kv_in,
    modulation_in,
    final_weight_in,
    mixed,
    flags,
    guide,
    frames,
    starts,
    video,
    image,
    audio_q,
    audio_kv,
    modulation,
    final_weight,
    loads,
    staged,
    staged_img,
    got,
    got_img,
    outs,
    back,
    gathered,
    audio_wide,
    audio_out,
    hidden,
    send_v,
    recv_v,
    send_i,
    recv_i,
    send_a,
    recv_a,
    send_b,
    recv_b,
    send_o,
    recv_o,
):
    heads, branches, rows, wide = video.shape
    dim = wide // 3
    img_rows = image.shape[2]
    inner = heads * dim
    units = heads * branches // n
    tokens = n * rows
    me = lax.axis_index("seq")
    bits = (n - 1).bit_length()
    flips = [(1 - 2 * ((me // 2**i) % 2)) * 2**i for i in range(bits)]

    def partner(k):
        other = me
        for i in range(bits):
            other = other + ((k // 2**i) % 2) * flips[i]
        return other

    def each_peer(body):
        def step(i, carry):
            body(partner(n - 1 - i))
            return carry

        lax.fori_loop(0, n - 1, step, 0)

    def send(src, dst, s_sem, r_sem, other):
        pltpu.make_async_remote_copy(
            src_ref=src,
            dst_ref=dst,
            send_sem=s_sem,
            recv_sem=r_sem,
            device_id={"seq": other},
            device_id_type=pl.DeviceIdType.MESH,
        ).start()

    def drain(ref, sem):
        pltpu.make_async_copy(ref, ref, sem).wait()

    pairs = (
        (flags_in, flags),
        (video_in, video),
        (image_in, image),
        (audio_kv_in, audio_kv),
        (frames_in, frames),
        (starts_in, starts),
        (guide_in, guide),
        (audio_q_in, audio_q),
        (modulation_in, modulation),
        (final_weight_in, final_weight),
    )
    fetches = [pltpu.make_async_copy(src, dst, loads.at[i]) for i, (src, dst) in enumerate(pairs)]
    for fetch in fetches:
        fetch.start()

    barrier = pltpu.get_barrier_semaphore()
    each_peer(
        lambda other: pl.semaphore_signal(
            barrier, inc=1, device_id={"seq": other}, device_id_type=pl.DeviceIdType.MESH
        )
    )

    for fetch in fetches[:4]:
        fetch.wait()
    place = []
    for aud, img in PAIRS:
        at = jnp.int32(0)
        for b in range(branches):
            f0, f1 = flags[0, b], flags[1, b]
            at = at + b * ((f0 if aud else 1 - f0) * (f1 if img else 1 - f1))
        place.append(jnp.minimum(at, branches - 1))

    def stage(h, carry):
        for p in range(branches):
            staged[h * branches + p] = video[h, place[p]]
        for p in range(0, branches, 2):
            staged_img[h * (branches // 2) + p // 2] = image[h, place[p]]
        return carry

    lax.fori_loop(0, heads, stage, 0)
    pl.semaphore_wait(barrier, n - 1)

    mine = pl.ds(pl.multiple_of(me * rows, rows), rows)
    mine_img = pl.ds(pl.multiple_of(me * img_rows, img_rows), img_rows)

    strips = n // plane
    my_strip, my_seat = me // plane, me % plane
    pltpu.sync_copy(audio_kv, gathered.at[my_seat, my_strip])

    def far(i, carry):
        strip = (my_strip + 1 + i) % strips
        send(
            audio_kv,
            gathered.at[my_seat, my_strip],
            send_a,
            recv_a,
            strip * plane + my_seat,
        )
        return carry

    lax.fori_loop(0, strips - 1, far, 0)

    def send_unit(j):
        each_peer(
            lambda other: send(
                staged.at[other * units + j], got.at[j, mine], send_v.at[j], recv_v.at[j], other
            )
        )

    def send_image(m):
        def one(other):
            if units > 1:
                item = other * (units // 2) + m
                send(staged_img.at[item], got_img.at[m, mine_img], send_i.at[m], recv_i.at[m], other)
            else:

                @pl.when(other % 2 == 0)
                def _():
                    send(
                        staged_img.at[other // 2],
                        got_img.at[m, mine_img],
                        send_i.at[m],
                        recv_i.at[m],
                        other,
                    )

        each_peer(one)

    send_unit(0)
    send_image(0)
    drain(gathered.at[0, pl.ds(0, strips - 1)], recv_a)

    def near(i, carry):
        seat = (my_seat + 1 + i) % plane
        send(
            gathered.at[my_seat], gathered.at[my_seat], send_b, recv_b, my_strip * plane + seat
        )
        return carry

    lax.fori_loop(0, plane - 1, near, 0)
    for j in range(1, units):
        send_unit(j)
        if j % 2 == 0:
            send_image(j // 2)

    for j in range(units):
        got[j, mine] = staged[me * units + j]
    if units > 1:
        for m in range(units // 2):
            got_img[m, mine_img] = staged_img[me * (units // 2) + m]
    else:

        @pl.when(me % 2 == 0)
        def _():
            got_img[0, mine_img] = staged_img[me // 2]

    for fetch in fetches[4:]:
        fetch.wait()
    spots = lax.broadcasted_iota(jnp.int32, (rows, 1), 0)

    def start_of(t, column):
        return jnp.where(spots == t, starts[frames[me * rows + t]], column)

    first = lax.fori_loop(0, rows, start_of, jnp.zeros((rows, 1), jnp.int32))
    audio_rows = audio_kv.shape[0]
    audio_count = n * audio_rows
    slots = lax.broadcasted_iota(jnp.int32, (rows, audio_count), 1)
    inside = (slots >= first) & (slots < first + AUD_WIN)
    ranks = audio_q.shape[0]
    inside = jnp.concatenate([inside] * ranks, axis=0)

    drain(gathered.at[pl.ds(0, plane - 1)], recv_b)
    per = 8 // audio_rows

    def widen(g, carry):
        pieces = []
        for i in range(per):
            src = g * per + i
            pieces.append(gathered[src % plane, src // plane].astype(jnp.float32))
        audio_wide[pl.ds(pl.multiple_of(g * 8, 8), 8), :] = jnp.concatenate(pieces, axis=0)
        return carry

    lax.fori_loop(0, audio_count // 8, widen, 0)
    scale = 1.0 / math.sqrt(dim)
    log2e = math.log2(math.e)
    transposed = (((1,), (1,)), ((), ()))

    def audio_head(h, carry):
        cols = pl.ds(pl.multiple_of(h * dim, dim), dim)
        val_cols = pl.ds(pl.multiple_of(inner + h * dim, dim), dim)
        q = audio_q[:, :, cols].reshape(ranks * rows, dim)
        k = audio_wide[:, cols].astype(jnp.bfloat16)
        v = audio_wide[:, val_cols].astype(jnp.bfloat16)
        s = lax.dot_general(q, k, transposed, preferred_element_type=jnp.float32)
        s = jnp.where(inside, s, -jnp.inf)
        top = jnp.max(s, axis=1, keepdims=True)
        w = jnp.where(inside, jnp.exp2((s - top) * (scale * log2e)), 0.0)
        total = jnp.sum(w, axis=1, keepdims=True)
        o = jnp.dot(w.astype(jnp.bfloat16), v, preferred_element_type=jnp.float32) / total
        audio_out[:, :, cols] = o.reshape(ranks, rows, dim)
        return carry

    lax.fori_loop(0, heads, audio_head, 0)

    blocks = tokens // q_block
    per_block = q_block // rows
    turn = me // per_block + 1

    def attend(j, with_image):
        def block(i, carry):
            b = (turn + i) % blocks
            at = pl.ds(pl.multiple_of(b * q_block, q_block), q_block)
            q = got[j, at, 0:dim]
            k = got[j, :, dim : 2 * dim]
            v = got[j, :, 2 * dim :]
            s = lax.dot_general(q, k, transposed, preferred_element_type=jnp.float32)
            top = jnp.max(s, axis=1, keepdims=True)
            if with_image:
                ki = got_img[j // 2, :, 0:dim]
                vi = got_img[j // 2, :, dim:]
                si = lax.dot_general(q, ki, transposed, preferred_element_type=jnp.float32)
                top = jnp.maximum(top, jnp.max(si, axis=1, keepdims=True))
            w = jnp.exp2((s - top) * (scale * log2e))
            total = jnp.sum(w, axis=1, keepdims=True)
            o = jnp.dot(w.astype(jnp.bfloat16), v, preferred_element_type=jnp.float32)
            if with_image:
                wi = jnp.exp2((si - top) * (scale * log2e))
                total = total + jnp.sum(wi, axis=1, keepdims=True)
                o = o + jnp.dot(wi.astype(jnp.bfloat16), vi, preferred_element_type=jnp.float32)
            outs[j, at, :] = (o / total).astype(jnp.bfloat16)

            def give(d, inner_carry):
                other = b * per_block + d
                part = outs.at[j, pl.ds(pl.multiple_of(other * rows, rows), rows)]

                @pl.when(other != me)
                def _():
                    send(part, back.at[j, me], send_o.at[j], recv_o.at[j], other)

                return inner_carry

            lax.fori_loop(0, per_block, give, 0)
            return carry

        lax.fori_loop(0, blocks, block, 0)
        back[j, me] = outs[j, mine, :]

    for j in range(units):
        drain(got.at[j, pl.ds(0, (n - 1) * rows)], recv_v.at[j])
        if units > 1:
            if j % 2 == 0:
                drain(got_img.at[j // 2, pl.ds(0, (n - 1) * img_rows)], recv_i.at[j // 2])
            attend(j, j % 2 == 0)
        else:

            @pl.when(me % 2 == 0)
            def _():
                drain(got_img.at[0, pl.ds(0, (n - 1) * img_rows)], recv_i.at[0])
                attend(0, True)

            @pl.when(me % 2 == 1)
            def _():
                attend(0, False)

    swapped = jnp.where(place[0] > place[1], 1, 0)
    seats = (swapped, 1 - swapped)
    result = jnp.zeros(mixed.shape, jnp.float32)
    for j in range(units):
        drain(back.at[j, pl.ds(0, n - 1)], recv_o.at[j])
        for p in range(j, branches, units):
            for h in range(heads):
                cols = slice(h * dim, (h + 1) * dim)
                x = back[j, (h * branches + p) // units].astype(jnp.float32)
                if PAIRS[p][0]:
                    x = x + audio_out[seats[p], :, cols]
                hidden[:, cols] = x
            x = hidden[...]
            center = jnp.mean(x, axis=1, keepdims=True)
            x = x - center
            spread = jnp.mean(jnp.square(x), axis=1, keepdims=True)
            x = x * lax.rsqrt(spread + 1e-06)
            gain = modulation[1, pl.ds(place[p], 1), :]
            shift = modulation[0, pl.ds(place[p], 1), :]
            x = (x * (1.0 + gain) + shift).astype(jnp.bfloat16)
            y = lax.dot_general(x, final_weight[...], transposed, preferred_element_type=jnp.float32)
            result = result + guide[place[p]].astype(jnp.float32) * y
    mixed[...] = result

    drain(gathered.at[0, pl.ds(0, strips - 1)], send_a)
    drain(gathered.at[pl.ds(0, plane - 1)], send_b)
    for j in range(units):
        drain(staged.at[pl.ds(0, n - 1)], send_v.at[j])
        drain(back.at[j, pl.ds(0, n - 1)], send_o.at[j])
    if units > 1:
        for m in range(units // 2):
            drain(staged_img.at[pl.ds(0, n - 1)], send_i.at[m])
    else:

        @pl.when(me % 2 == 0)
        def _():
            drain(staged_img.at[pl.ds(0, n // 2 - 1)], send_i.at[0])

        @pl.when(me % 2 == 1)
        def _():
            drain(staged_img.at[pl.ds(0, n // 2)], send_i.at[0])


def shards(
    video_heads,
    image_heads,
    audio_queries,
    audio_keys,
    condition_flags,
    guidance_weights,
    token_frame,
    window_start,
    modulation,
    final_weight,
    noisy_latent,
):
    heads, branches, rows, wide = video_heads.shape
    dim = wide // 3
    img_rows = image_heads.shape[2]
    n = lax.axis_size("seq")
    units = heads * branches // n
    assert n & (n - 1) == 0 and units in (1, 2, 4)
    bits = (n - 1).bit_length()
    plane = 2 ** ((bits + 1) // 2)
    tokens = n * rows
    q_block = min(256, tokens)
    images = max(1, units // 2)
    inner = heads * dim
    bf16, f32 = jnp.bfloat16, jnp.float32
    dma = pltpu.SemaphoreType.DMA
    def like(x, space):
        return space(x.shape, x.dtype)

    columns = final_weight.T
    small = (condition_flags, guidance_weights, token_frame, window_start)
    large = (video_heads, image_heads, audio_queries, audio_keys, modulation, columns)
    mixed = pl.pallas_call(
        functools.partial(step_kernel, n, q_block, plane),
        out_shape=jax.ShapeDtypeStruct(noisy_latent.shape, f32),
        in_specs=[pl.BlockSpec(memory_space=pl.ANY)] * (len(small) + len(large)),
        out_specs=pl.BlockSpec(memory_space=pltpu.VMEM),
        scratch_shapes=[
            *[like(x, pltpu.SMEM) for x in small],
            *[like(x, pltpu.VMEM) for x in large],
            dma((len(small) + len(large),)),
            pltpu.VMEM((heads * branches, rows, wide), bf16),
            pltpu.VMEM((heads * branches // 2, img_rows, 2 * dim), bf16),
            pltpu.VMEM((units, tokens, wide), bf16),
            pltpu.VMEM((images, n * img_rows, 2 * dim), bf16),
            pltpu.VMEM((units, tokens, dim), bf16),
            pltpu.VMEM((units, n, rows, dim), bf16),
            pltpu.VMEM((plane, n // plane) + audio_keys.shape, bf16),
            pltpu.VMEM((n * audio_keys.shape[0], 2 * inner), f32),
            pltpu.VMEM((audio_queries.shape[0], rows, inner), f32),
            pltpu.VMEM((rows, inner), f32),
            dma((units,)),
            dma((units,)),
            dma((images,)),
            dma((images,)),
            dma,
            dma,
            dma,
            dma,
            dma((units,)),
            dma((units,)),
        ],
        compiler_params=pltpu.CompilerParams(
            collective_id=0, has_side_effects=True, vmem_limit_bytes=67043328
        ),
        name="avatar_step",
    )(*small, *large)
    velocity = mixed / 8.0
    return (velocity, noisy_latent - 0.125 * velocity)


def solution(mesh):
    in_specs = (
        P("groups", None, "seq", None),
        P("groups", None, "seq", None),
        P("groups", "seq", None),
        P("seq", "groups"),
        P("groups", None),
        P("groups"),
        P("groups"),
        P("groups"),
        P("groups", None, None),
        P(),
        P(("groups", "seq"), None),
    )
    out_specs = (P(("groups", "seq"), None), P(("groups", "seq"), None))
    return jax.shard_map(shards, mesh=mesh, in_specs=in_specs, out_specs=out_specs, check_vma=False)
```

profile of v0, /device:TPU:0, one launch (start us, length us, event | category | flops | bytes accessed | tf_op | source)
XLA Modules:
  0.0 61.8 jit_solution(15864930538701136884)
XLA Ops:
  0.6 59.8 %avatar_step.1 = f32[32,64]{1,0:T(8,128)} custom-call(s32[2,4]{1,0:T(2,128)} %flags_in.1, s32[4]{0:T(128)} %guide_in.1, s32[1024]{0:T(1024)} %frames_in.1, s32[16]{0:T(128)} %starts_in.1, bf16[16,4,32,384]{3,2,1,0:T(8,128)(2,1)} %video_in.1, bf16[16,4,16,256]{3,2,1,0:T(8,128)(2,1)} %image_in.1, bf16[2,32,2048]{2,1,0:T(8,128)(2,1)} %audio_q_in.1, ...), custom_call_target="tpu_custom_call" | custom-call | tf_op jit(solution)/shard_map/avatar_step/pallas_call | solution.py:399
  60.4 1.4 %multiply_subtract_fusion = (f32[32,64]{1,0:T(8,128)}, f32[32,64]{1,0:T(8,128)}) fusion(f32[32,64]{1,0:T(8,128)} %param.21, f32[32,64]{1,0:T(8,128)} %avatar_step.1), kind=kLoop, calls=%fused_computation | loop fusion | flops 6144 | bytes 32768 | tf_op jit(solution)/shard_map/sub | solution.py:435
where the time goes:
time: 62.3 us; the launch traced here: 61.8 us
  Pallas kernels  59.8 us (96%)
  other arithmetic  1.35 us (2%)
  between operations  0.64 us (1%)
    pallas_call x1, Pallas kernels, shards(): pl.pallas_call(functools.partial(step_kernel, n, q_block, plane), out_sha...  59.8 us
    sub x1, other arithmetic, shards(): return (velocity, noisy_latent - 0.125 * velocity)  1.35 us

commit v1 on v0

--- a/solution.py
+++ b/solution.py
@@ -363,6 +363,363 @@
             drain(staged_img.at[pl.ds(0, n // 2)], send_i.at[0])
 
 
+def split_kernel(
+    n,
+    q_block,
+    plane,
+    flags_in,
+    guide_in,
+    frames_in,
+    starts_in,
+    video_in,
+    image_in,
+    audio_q_in,
+    audio_kv_in,
+    modulation_in,
+    final_weight_in,
+    mixed,
+    flags,
+    guide,
+    frames,
+    starts,
+    video,
+    image,
+    audio_q,
+    audio_kv,
+    modulation,
+    final_weight,
+    loads,
+    st_q,
+    st_k,
+    st_c,
+    got_q,
+    got_k,
+    got_c,
+    out_b,
+    out_s,
+    out_c,
+    back_b,
+    back_s,
+    back_c,
+    gathered,
+    audio_wide,
+    audio_out,
+    hidden,
+    weights,
+    sends,
+    recvs,
+):
+    heads, branches, rows, wide = video.shape
+    dim = wide // 3
+    img_rows = image.shape[2]
+    inner = heads * dim
+    half = n // 2
+    me = lax.axis_index("seq")
+    loc = me % half
+    bits = (n - 1).bit_length()
+    flips = [(1 - 2 * ((me // 2**i) % 2)) * 2**i for i in range(bits)]
+
+    def partner(k):
+        other = me
+        for i in range(bits):
+            other = other + ((k // 2**i) % 2) * flips[i]
+        return other
+
+    def loop(count, body):
+        def step(i, carry):
+            body(i)
+            return carry
+
+        lax.fori_loop(0, count, step, 0)
+
+    def send(src, dst, which, other):
+        pltpu.make_async_remote_copy(
+            src_ref=src,
+            dst_ref=dst,
+            send_sem=sends.at[which],
+            recv_sem=recvs.at[which],
+            device_id={"seq": other},
+            device_id_type=pl.DeviceIdType.MESH,
+        ).start()
+
+    def drain(ref, sem):
+        pltpu.make_async_copy(ref, ref, sem).wait()
+
+    Q, K, C, FAR, NEAR, RB, RS, RC = range(8)
+
+    barrier = pltpu.get_barrier_semaphore()
+    loop(
+        n - 1,
+        lambda i: pl.semaphore_signal(
+            barrier, inc=1, device_id={"seq": partner(n - 1 - i)}, device_id_type=pl.DeviceIdType.MESH
+        ),
+    )
+    pairs = (
+        (flags_in, flags),
+        (video_in, video),
+        (image_in, image),
+        (audio_kv_in, audio_kv),
+        (frames_in, frames),
+        (starts_in, starts),
+        (guide_in, guide),
+        (audio_q_in, audio_q),
+        (modulation_in, modulation),
+        (final_weight_in, final_weight),
+    )
+    fetches = [pltpu.make_async_copy(src, dst, loads.at[i]) for i, (src, dst) in enumerate(pairs)]
+    for fetch in fetches:
+        fetch.start()
+    for fetch in fetches[:4]:
+        fetch.wait()
+    place = []
+    for aud, img in PAIRS:
+        at = jnp.int32(0)
+        for b in range(branches):
+            f0, f1 = flags[0, b], flags[1, b]
+            at = at + b * ((f0 if aud else 1 - f0) * (f1 if img else 1 - f1))
+        place.append(jnp.minimum(at, branches - 1))
+
+    def stage(h):
+        for j in range(2):
+            x = video[h, place[2 * j]]
+            st_q[h, :, j * dim : (j + 1) * dim] = x[:, :dim]
+            st_k[h, :, 2 * j * dim : 2 * (j + 1) * dim] = x[:, dim:]
+            st_k[h, j * img_rows : (j + 1) * img_rows, 4 * dim :] = image[h, place[2 * j]]
+            st_c[2 * h + j] = video[h, place[2 * j + 1]]
+
+    loop(heads, stage)
+    pl.semaphore_wait(barrier, n - 1)
+
+    strips = n // plane
+    my_strip, my_seat = me // plane, me % plane
+    pltpu.sync_copy(audio_kv, gathered.at[my_seat, my_strip])
+
+    def far(i):
+        strip = (my_strip + 1 + i) % strips
+        send(audio_kv, gathered.at[my_seat, my_strip], FAR, strip * plane + my_seat)
+
+    loop(strips - 1, far)
+
+    def send_q(other):
+        send(st_q.at[other % half], got_q.at[me], Q, other)
+
+    def send_k(other):
+        send(st_k.at[other % half], got_k.at[loc], K, other)
+
+    def send_c(other):
+        send(st_c.at[other], got_c.at[me], C, other)
+
+    def first(i):
+        send_q(partner(n - 1 - i))
+
+        @pl.when(i < half - 1)
+        def _():
+            other = partner(half - 1 - i)
+            send_k(other)
+            send_q(other)
+
+    loop(half, first)
+    drain(gathered.at[0, pl.ds(0, strips - 1)], recvs.at[FAR])
+
+    def near(i):
+        seat = (my_seat + 1 + i) % plane
+        send(gathered.at[my_seat], gathered.at[my_seat], NEAR, my_strip * plane + seat)
+
+    loop(plane - 1, near)
+
+    def second(i):
+        send_c(partner(n - 1 - i))
+
+        @pl.when(i < half - 1)
+        def _():
+            send_c(partner(half - 1 - i))
+
+    loop(half, second)
+
+    got_q[me] = st_q[loc]
+    got_k[loc] = st_k[loc]
+    got_c[me] = st_c[me]
+
+    scale = 1.0 / math.sqrt(dim)
+    rate = scale * math.log2(math.e)
+    transposed = (((1,), (1,)), ((), ()))
+
+    blocks = n * rows // q_block
+    per_block = q_block // rows
+    turn = me // per_block + 1
+
+    def attend(q, keys, values):
+        scores = [lax.dot_general(q, k, transposed, preferred_element_type=jnp.float32) for k in keys]
+        top = functools.reduce(jnp.maximum, [jnp.max(s, axis=1, keepdims=True) for s in scores])
+        total, o = 0.0, 0.0
+        for s, v in zip(scores, values):
+            w = jnp.exp2((s - top) * rate)
+            total = total + jnp.sum(w, axis=1, keepdims=True)
+            o = o + jnp.dot(w.astype(jnp.bfloat16), v, preferred_element_type=jnp.float32)
+        return (o / total).astype(jnp.bfloat16), top, total
+
+    def give(b, body):
+        def one(d):
+            other = b * per_block + d
+
+            @pl.when(other != me)
+            def _():
+                body(other)
+
+        loop(per_block, one)
+
+    drain(got_q.at[pl.ds(0, n - 1)], recvs.at[Q])
+    drain(got_k.at[pl.ds(0, half - 1)], recvs.at[K])
+
+    lane = lax.broadcasted_iota(jnp.int32, (q_block, 4 * rows), 1)
+    diagonal = lane % rows == lax.broadcasted_iota(jnp.int32, (q_block, 4 * rows), 0) % rows
+
+    def image_block(i):
+        b = (turn + i) % blocks
+        devices = pl.ds(pl.multiple_of(b * per_block, per_block), per_block)
+        stats = []
+        for j in range(2):
+            q = got_q[devices, :, j * dim : (j + 1) * dim].reshape(q_block, dim)
+            at = 2 * j * dim
+            k = got_k[:, :, at : at + dim].reshape(half * rows, dim)
+            v = got_k[:, :, at + dim : at + 2 * dim].reshape(half * rows, dim)
+            pick = slice(j * img_rows, (j + 1) * img_rows)
+            ki = got_k[:, pick, 4 * dim : 5 * dim].reshape(half * img_rows, dim)
+            vi = got_k[:, pick, 5 * dim :].reshape(half * img_rows, dim)
+            o, top, total = attend(q, (k, ki), (v, vi))
+            out_b[devices, :, j * dim : (j + 1) * dim] = o.reshape(per_block, rows, dim)
+            stats += [top, total]
+        x = jnp.where(lane < rows, stats[0], jnp.where(lane < 2 * rows, stats[1], jnp.where(lane < 3 * rows, stats[2], stats[3])))
+        x = jnp.where(diagonal, x, 0.0).reshape(per_block, rows, 4 * rows)
+        out_s[devices, 0, :] = jnp.sum(x, axis=1)
+
+        def body(other):
+            send(out_b.at[other], back_b.at[me], RB, other)
+            send(out_s.at[other], back_s.at[me], RS, other)
+
+        give(b, body)
+
+    loop(blocks, image_block)
+    back_b[me] = out_b[me]
+    back_s[me] = out_s[me]
+
+    for fetch in fetches[4:]:
+        fetch.wait()
+    spots = lax.broadcasted_iota(jnp.int32, (rows, 1), 0)
+
+    def start_of(t, column):
+        return jnp.where(spots == t, starts[frames[me * rows + t]], column)
+
+    begin = lax.fori_loop(0, rows, start_of, jnp.zeros((rows, 1), jnp.int32))
+    audio_rows = audio_kv.shape[0]
+    audio_count = n * audio_rows
+    slots = lax.broadcasted_iota(jnp.int32, (rows, audio_count), 1)
+    inside = (slots >= begin) & (slots < begin + AUD_WIN)
+    ranks = audio_q.shape[0]
+    inside = jnp.concatenate([inside] * ranks, axis=0)
+
+    drain(gathered.at[pl.ds(0, plane - 1)], recvs.at[NEAR])
+    per = 8 // audio_rows
+
+    def widen(g):
+        pieces = []
+        for i in range(per):
+            src = g * per + i
+            pieces.append(gathered[src % plane, src // plane].astype(jnp.float32))
+        audio_wide[pl.ds(pl.multiple_of(g * 8, 8), 8), :] = jnp.concatenate(pieces, axis=0)
+
+    loop(audio_count // 8, widen)
+    def audio_head(h):
+        cols = pl.ds(pl.multiple_of(h * dim, dim), dim)
+        val_cols = pl.ds(pl.multiple_of(inner + h * dim, dim), dim)
+        q = audio_q[:, :, cols].reshape(ranks * rows, dim)
+        k = audio_wide[:, cols].astype(jnp.bfloat16)
+        v = audio_wide[:, val_cols].astype(jnp.bfloat16)
+        s = lax.dot_general(q, k, transposed, preferred_element_type=jnp.float32)
+        s = jnp.where(inside, s, -jnp.inf)
+        top = jnp.max(s, axis=1, keepdims=True)
+        w = jnp.where(inside, jnp.exp2((s - top) * rate), 0.0)
+        total = jnp.sum(w, axis=1, keepdims=True)
+        o = jnp.dot(w.astype(jnp.bfloat16), v, preferred_element_type=jnp.float32) / total
+        audio_out[:, :, cols] = o.reshape(ranks, rows, dim)
+
+    loop(heads, audio_head)
+
+    drain(got_c.at[pl.ds(0, n - 1)], recvs.at[C])
+
+    def plain_block(i):
+        b = (turn + i) % blocks
+        devices = pl.ds(pl.multiple_of(b * per_block, per_block), per_block)
+        q = got_c[devices, :, 0:dim].reshape(q_block, dim)
+        k = got_c[:, :, dim : 2 * dim].reshape(n * rows, dim)
+        v = got_c[:, :, 2 * dim :].reshape(n * rows, dim)
+        o, _, _ = attend(q, (k,), (v,))
+        out_c[devices] = o.reshape(per_block, rows, dim)
+        give(b, lambda other: send(out_c.at[other], back_c.at[me], RC, other))
+
+    loop(blocks, plain_block)
+    back_c[me] = out_c[me]
+
+    swapped = jnp.where(place[0] > place[1], 1, 0)
+    seats = (swapped, 1 - swapped)
+
+    def finish(p, result):
+        x = hidden[...]
+        center = jnp.mean(x, axis=1, keepdims=True)
+        x = x - center
+        spread = jnp.mean(jnp.square(x), axis=1, keepdims=True)
+        x = x * lax.rsqrt(spread + 1e-06)
+        gain = modulation[1, pl.ds(place[p], 1), :]
+        shift = modulation[0, pl.ds(place[p], 1), :]
+        x = (x * (1.0 + gain) + shift).astype(jnp.bfloat16)
+        y = lax.dot_general(x, final_weight[...], transposed, preferred_element_type=jnp.float32)
+        return result + guide[place[p]].astype(jnp.float32) * y
+
+    result = jnp.zeros(mixed.shape, jnp.float32)
+    drain(back_b.at[pl.ds(0, n - 1)], recvs.at[RB])
+    drain(back_s.at[pl.ds(0, n - 1)], recvs.at[RS])
+    a, b = back_s[0:half, 0, :], back_s[half:n, 0, :]
+    most = jnp.maximum(a, b)
+    lanes = 4 * rows
+    a = jnp.exp2((a - most) * rate) * pltpu.roll(a, lanes - rows, 1)
+    b = jnp.exp2((b - most) * rate) * pltpu.roll(b, lanes - rows, 1)
+    whole = a + b
+    parts = [a / whole, b / whole, jnp.zeros((lanes - n, lanes), jnp.float32)]
+    weights[...] = jnp.concatenate(parts, axis=0).T
+    for j in range(2):
+        p = 2 * j
+        tokens = slice(2 * j * rows, (2 * j + 1) * rows)
+        for h in range(heads):
+            cols = slice(h * dim, (h + 1) * dim)
+            x = weights[tokens, h : h + 1] * back_b[h, :, j * dim : (j + 1) * dim].astype(jnp.float32)
+            other = half + h
+            x = x + weights[tokens, other : other + 1] * back_b[other, :, j * dim : (j + 1) * dim].astype(jnp.float32)
+            if PAIRS[p][0]:
+                x = x + audio_out[seats[p], :, cols]
+            hidden[:, cols] = x
+        result = finish(p, result)
+    drain(back_c.at[pl.ds(0, n - 1)], recvs.at[RC])
+    for j in range(2):
+        p = 2 * j + 1
+        for h in range(heads):
+            cols = slice(h * dim, (h + 1) * dim)
+            x = back_c[2 * h + j].astype(jnp.float32)
+            if PAIRS[p][0]:
+                x = x + audio_out[seats[p], :, cols]
+            hidden[:, cols] = x
+        result = finish(p, result)
+    mixed[...] = result
+
+    drain(gathered.at[0, pl.ds(0, strips - 1)], sends.at[FAR])
+    drain(gathered.at[pl.ds(0, plane - 1)], sends.at[NEAR])
+    drain(got_q.at[pl.ds(0, n - 1)], sends.at[Q])
+    drain(got_k.at[pl.ds(0, half - 1)], sends.at[K])
+    drain(got_c.at[pl.ds(0, n - 1)], sends.at[C])
+    drain(back_b.at[pl.ds(0, n - 1)], sends.at[RB])
+    drain(back_s.at[pl.ds(0, n - 1)], sends.at[RS])
+    drain(back_c.at[pl.ds(0, n - 1)], sends.at[RC])
+
+
 def shards(
     video_heads,
     image_heads,
@@ -396,15 +753,33 @@
     columns = final_weight.T
     small = (condition_flags, guidance_weights, token_frame, window_start)
     large = (video_heads, image_heads, audio_queries, audio_keys, modulation, columns)
-    mixed = pl.pallas_call(
-        functools.partial(step_kernel, n, q_block, plane),
-        out_shape=jax.ShapeDtypeStruct(noisy_latent.shape, f32),
-        in_specs=[pl.BlockSpec(memory_space=pl.ANY)] * (len(small) + len(large)),
-        out_specs=pl.BlockSpec(memory_space=pltpu.VMEM),
-        scratch_shapes=[
-            *[like(x, pltpu.SMEM) for x in small],
-            *[like(x, pltpu.VMEM) for x in large],
-            dma((len(small) + len(large),)),
+    if 2 * heads == n and branches == 4 and 4 * rows == 128 and rows == 2 * img_rows:
+        half = n // 2
+        kernel = split_kernel
+        working = [
+            pltpu.VMEM((heads, rows, 2 * dim), bf16),
+            pltpu.VMEM((heads, rows, 6 * dim), bf16),
+            pltpu.VMEM((n, rows, wide), bf16),
+            pltpu.VMEM((n, rows, 2 * dim), bf16),
+            pltpu.VMEM((half, rows, 6 * dim), bf16),
+            pltpu.VMEM((n, rows, wide), bf16),
+            pltpu.VMEM((n, rows, 2 * dim), bf16),
+            pltpu.VMEM((n, 1, 4 * rows), f32),
+            pltpu.VMEM((n, rows, dim), bf16),
+            pltpu.VMEM((n, rows, 2 * dim), bf16),
+            pltpu.VMEM((n, 1, 4 * rows), f32),
+            pltpu.VMEM((n, rows, dim), bf16),
+            pltpu.VMEM((plane, n // plane) + audio_keys.shape, bf16),
+            pltpu.VMEM((n * audio_keys.shape[0], 2 * inner), f32),
+            pltpu.VMEM((audio_queries.shape[0], rows, inner), f32),
+            pltpu.VMEM((rows, inner), f32),
+            pltpu.VMEM((4 * rows, 4 * rows), f32),
+            dma((8,)),
+            dma((8,)),
+        ]
+    else:
+        kernel = step_kernel
+        working = [
             pltpu.VMEM((heads * branches, rows, wide), bf16),
             pltpu.VMEM((heads * branches // 2, img_rows, 2 * dim), bf16),
             pltpu.VMEM((units, tokens, wide), bf16),
@@ -425,6 +800,17 @@
             dma,
             dma((units,)),
             dma((units,)),
+        ]
+    mixed = pl.pallas_call(
+        functools.partial(kernel, n, q_block, plane),
+        out_shape=jax.ShapeDtypeStruct(noisy_latent.shape, f32),
+        in_specs=[pl.BlockSpec(memory_space=pl.ANY)] * (len(small) + len(large)),
+        out_specs=pl.BlockSpec(memory_space=pltpu.VMEM),
+        scratch_shapes=[
+            *[like(x, pltpu.SMEM) for x in small],
+            *[like(x, pltpu.VMEM) for x in large],
+            dma((len(small) + len(large),)),
+            *working,
         ],
         compiler_params=pltpu.CompilerParams(
             collective_id=0, has_side_effects=True, vmem_limit_bytes=67043328

time: 62.3 us -> 58.6 us (0.941)
  Pallas kernels: 59.8 us -> 56.3 us
    pallas_call x1, Pallas kernels: 59.8 us -> 56.3 us  [shards(): pl.pallas_call(functools.partial(kernel, n, q_block, plane), out_shape=ja...]
where the time goes in v1:
time: 58.6 us; the launch traced here: 58.3 us
  Pallas kernels  56.3 us (96%)
  other arithmetic  1.35 us (2%)
  between operations  0.64 us (1%)
    pallas_call x1, Pallas kernels, shards(): pl.pallas_call(functools.partial(kernel, n, q_block, plane), out_shape=ja...  56.3 us
    sub x1, other arithmetic, shards(): return (velocity, noisy_latent - 0.125 * velocity)  1.35 us

profile of v1, /device:TPU:0, one launch (start us, length us, event | category | flops | bytes accessed | tf_op | source)
XLA Modules:
  0.0 58.3 jit_solution(2769375644231145937)
XLA Ops:
  0.6 56.3 %avatar_step.1 = f32[32,64]{1,0:T(8,128)} custom-call(s32[2,4]{1,0:T(2,128)} %flags_in.1, s32[4]{0:T(128)} %guide_in.1, s32[1024]{0:T(1024)} %frames_in.1, s32[16]{0:T(128)} %starts_in.1, bf16[16,4,32,384]{3,2,1,0:T(8,128)(2,1)} %video_in.1, bf16[16,4,16,256]{3,2,1,0:T(8,128)(2,1)} %image_in.1, bf16[2,32,2048]{2,1,0:T(8,128)(2,1)} %audio_q_in.1, ...), custom_call_target="tpu_custom_call" | custom-call | tf_op jit(solution)/shard_map/avatar_step/pallas_call | solution.py:804
  57.0 1.4 %multiply_subtract_fusion = (f32[32,64]{1,0:T(8,128)}, f32[32,64]{1,0:T(8,128)}) fusion(f32[32,64]{1,0:T(8,128)} %param.21, f32[32,64]{1,0:T(8,128)} %avatar_step.1), kind=kLoop, calls=%fused_computation | loop fusion | flops 6144 | bytes 32768 | tf_op jit(solution)/shard_map/sub | solution.py:821

commit v2 on v1

--- a/solution.py
+++ b/solution.py
@@ -398,22 +398,30 @@
     out_b,
     out_s,
     out_c,
+    out_y,
+    out_z,
     back_b,
     back_s,
     back_c,
+    back_y,
+    back_z,
     gathered,
     audio_wide,
     audio_out,
     hidden,
     weights,
+    folded,
     sends,
     recvs,
+    ready,
 ):
     heads, branches, rows, wide = video.shape
     dim = wide // 3
     img_rows = image.shape[2]
     inner = heads * dim
     half = n // 2
+    quarter = n // 4
+    channels = final_weight.shape[0]
     me = lax.axis_index("seq")
     loc = me % half
     bits = (n - 1).bit_length()
@@ -445,15 +453,22 @@
     def drain(ref, sem):
         pltpu.make_async_copy(ref, ref, sem).wait()
 
-    Q, K, C, FAR, NEAR, RB, RS, RC = range(8)
+    Q, K, C, FAR, NEAR, RB, RS, RC, RY, RZ = range(10)
+
+    central = (me >= quarter) & (me < half + quarter)
+    my_head = jnp.where(central, me - quarter, jnp.where(me < quarter, me, me - half))
+
+    kin = [k for k in range(n - 1, 0, -1) if k < plane or k % plane < 2]
+    rest = [k for k in range(n - 1, 0, -1) if k not in kin]
+
+    def greet(sem):
+        for k in kin:
+            pl.semaphore_signal(
+                sem, inc=1, device_id={"seq": partner(k)}, device_id_type=pl.DeviceIdType.MESH
+            )
 
     barrier = pltpu.get_barrier_semaphore()
-    loop(
-        n - 1,
-        lambda i: pl.semaphore_signal(
-            barrier, inc=1, device_id={"seq": partner(n - 1 - i)}, device_id_type=pl.DeviceIdType.MESH
-        ),
-    )
+    greet(barrier)
     pairs = (
         (flags_in, flags),
         (video_in, video),
@@ -485,10 +500,12 @@
             st_q[h, :, j * dim : (j + 1) * dim] = x[:, :dim]
             st_k[h, :, 2 * j * dim : 2 * (j + 1) * dim] = x[:, dim:]
             st_k[h, j * img_rows : (j + 1) * img_rows, 4 * dim :] = image[h, place[2 * j]]
-            st_c[2 * h + j] = video[h, place[2 * j + 1]]
+        st_c[quarter + h] = video[h, place[1]]
+        st_c[h + jnp.where(h < quarter, 0, half)] = video[h, place[3]]
 
     loop(heads, stage)
-    pl.semaphore_wait(barrier, n - 1)
+    pl.semaphore_wait(barrier, len(kin))
+    greet(ready)
 
     strips = n // plane
     my_strip, my_seat = me // plane, me % plane
@@ -509,16 +526,21 @@
     def send_c(other):
         send(st_c.at[other], got_c.at[me], C, other)
 
-    def first(i):
-        send_q(partner(n - 1 - i))
-
-        @pl.when(i < half - 1)
-        def _():
-            other = partner(half - 1 - i)
-            send_k(other)
+    def mixed_order(ks):
+        cross, same = [k for k in ks if k >= half], [k for k in ks if k < half]
+        for i in range(max(len(cross), len(same))):
+            yield from cross[i : i + 1] + same[i : i + 1]
+
+    def first(ks):
+        for k in mixed_order(ks):
+            other = partner(k)
+            if k < half:
+                send_k(other)
             send_q(other)
 
-    loop(half, first)
+    first(kin)
+    pl.semaphore_wait(ready, len(kin))
+    first(rest)
     drain(gathered.at[0, pl.ds(0, strips - 1)], recvs.at[FAR])
 
     def near(i):
@@ -530,11 +552,7 @@
     def second(i):
         send_c(partner(n - 1 - i))
 
-        @pl.when(i < half - 1)
-        def _():
-            send_c(partner(half - 1 - i))
-
-    loop(half, second)
+    loop(n - 1, second)
 
     got_q[me] = st_q[loc]
     got_k[loc] = st_k[loc]
@@ -568,11 +586,25 @@
 
         loop(per_block, one)
 
+    for fetch in fetches[4:]:
+        fetch.wait()
     drain(got_q.at[pl.ds(0, n - 1)], recvs.at[Q])
     drain(got_k.at[pl.ds(0, half - 1)], recvs.at[K])
 
     lane = lax.broadcasted_iota(jnp.int32, (q_block, 4 * rows), 1)
     diagonal = lane % rows == lax.broadcasted_iota(jnp.int32, (q_block, 4 * rows), 0) % rows
+
+    head_of = lax.broadcasted_iota(jnp.int32, (folded.shape[0], inner), 1) // dim
+    line = lax.broadcasted_iota(jnp.int32, (folded.shape[0], inner), 0)
+    gains = 1.0 + modulation[1, pl.ds(place[3], 1), :]
+    table = jnp.where(line == head_of, gains, jnp.where(line == heads, modulation[0, pl.ds(place[3], 1), :], 0.0))
+    folded[...] = lax.dot_general(
+        table,
+        final_weight[...].astype(jnp.float32),
+        transposed,
+        precision=lax.Precision.HIGHEST,
+        preferred_element_type=jnp.float32,
+    )
 
     def image_block(i):
         b = (turn + i) % blocks
@@ -603,8 +635,6 @@
     back_b[me] = out_b[me]
     back_s[me] = out_s[me]
 
-    for fetch in fetches[4:]:
-        fetch.wait()
     spots = lax.broadcasted_iota(jnp.int32, (rows, 1), 0)
 
     def start_of(t, column):
@@ -643,7 +673,7 @@
         o = jnp.dot(w.astype(jnp.bfloat16), v, preferred_element_type=jnp.float32) / total
         audio_out[:, :, cols] = o.reshape(ranks, rows, dim)
 
-    loop(heads, audio_head)
+    loop(heads // 2, audio_head)
 
     drain(got_c.at[pl.ds(0, n - 1)], recvs.at[C])
 
@@ -654,12 +684,48 @@
         k = got_c[:, :, dim : 2 * dim].reshape(n * rows, dim)
         v = got_c[:, :, 2 * dim :].reshape(n * rows, dim)
         o, _, _ = attend(q, (k,), (v,))
-        out_c[devices] = o.reshape(per_block, rows, dim)
-        give(b, lambda other: send(out_c.at[other], back_c.at[me], RC, other))
+
+        @pl.when(central)
+        def _():
+            out_c[devices] = o.reshape(per_block, rows, dim)
+            give(b, lambda other: send(out_c.at[other], back_c.at[my_head], RC, other))
+
+        @pl.when(jnp.logical_not(central))
+        def _():
+            x = o.astype(jnp.float32)
+            center = jnp.mean(x, axis=1, keepdims=True)
+            x = x - center
+            spread = jnp.sum(jnp.square(x), axis=1, keepdims=True)
+            cols = pl.ds(pl.multiple_of(my_head * dim, dim), dim)
+            chosen = lax.broadcasted_iota(jnp.int32, (branches, dim), 0) == place[3]
+            gain = jnp.sum(jnp.where(chosen, modulation[1, :, cols], 0.0), axis=0, keepdims=True)
+            x = (x * (1.0 + gain)).astype(jnp.bfloat16)
+            y = lax.dot_general(x, final_weight[:, cols], transposed, preferred_element_type=jnp.float32)
+            y = y.reshape(per_block, rows, channels)
+            y = jnp.concatenate([y[:, : rows // 2], y[:, rows // 2 :]], axis=2)
+            out_y[devices] = y.astype(jnp.bfloat16)
+            z = jnp.where(lane < rows, center, jnp.where(lane < 2 * rows, spread, 0.0))
+            z = jnp.where(diagonal, z, 0.0).reshape(per_block, rows, 4 * rows)
+            out_z[devices, 0, :] = jnp.sum(z, axis=1)
+
+            def body(other):
+                send(out_y.at[other], back_y.at[my_head], RY, other)
+                send(out_z.at[other], back_z.at[my_head], RZ, other)
+
+            give(b, body)
 
     loop(blocks, plain_block)
-    back_c[me] = out_c[me]
-
+
+    @pl.when(central)
+    def _():
+        back_c[my_head] = out_c[me]
+
+    @pl.when(jnp.logical_not(central))
+    def _():
+        back_y[my_head] = out_y[me]
+        back_z[my_head] = out_z[me]
+
+    loop(heads - heads // 2, lambda i: audio_head(heads // 2 + i))
     swapped = jnp.where(place[0] > place[1], 1, 0)
     seats = (swapped, 1 - swapped)
 
@@ -698,16 +764,35 @@
                 x = x + audio_out[seats[p], :, cols]
             hidden[:, cols] = x
         result = finish(p, result)
-    drain(back_c.at[pl.ds(0, n - 1)], recvs.at[RC])
-    for j in range(2):
-        p = 2 * j + 1
-        for h in range(heads):
-            cols = slice(h * dim, (h + 1) * dim)
-            x = back_c[2 * h + j].astype(jnp.float32)
-            if PAIRS[p][0]:
-                x = x + audio_out[seats[p], :, cols]
-            hidden[:, cols] = x
-        result = finish(p, result)
+
+    @pl.when(central)
+    def _():
+        drain(back_c.at[pl.ds(0, heads - 1)], recvs.at[RC])
+        drain(back_y, recvs.at[RY])
+        drain(back_z, recvs.at[RZ])
+
+    @pl.when(jnp.logical_not(central))
+    def _():
+        drain(back_c, recvs.at[RC])
+        drain(back_y.at[pl.ds(0, heads - 1)], recvs.at[RY])
+        drain(back_z.at[pl.ds(0, heads - 1)], recvs.at[RZ])
+
+    for h in range(heads):
+        cols = slice(h * dim, (h + 1) * dim)
+        hidden[:, cols] = back_c[h].astype(jnp.float32) + audio_out[seats[1], :, cols]
+    result = finish(1, result)
+    z = back_z[:, 0, :]
+    center = jnp.mean(z, axis=0, keepdims=True)
+    away = z - center
+    spread = jnp.sum(pltpu.roll(z, lanes - rows, 1) + dim * jnp.square(away), axis=0, keepdims=True) / inner
+    parts = [away, lax.rsqrt(spread + 1e-06), jnp.zeros((lanes - heads - 1, lanes), jnp.float32)]
+    weights[...] = jnp.concatenate(parts, axis=0).T
+    y = functools.reduce(jnp.add, [back_y[h].astype(jnp.float32) for h in range(heads)])
+    y = jnp.concatenate([y[:, :channels], y[:, channels:]], axis=0)
+    for h in range(heads):
+        y = y + weights[0:rows, h : h + 1] * folded[h : h + 1, :]
+    y = weights[0:rows, heads : heads + 1] * y + folded[heads : heads + 1, :]
+    result = result + guide[place[3]].astype(jnp.float32) * y
     mixed[...] = result
 
     drain(gathered.at[0, pl.ds(0, strips - 1)], sends.at[FAR])
@@ -717,7 +802,15 @@
     drain(got_c.at[pl.ds(0, n - 1)], sends.at[C])
     drain(back_b.at[pl.ds(0, n - 1)], sends.at[RB])
     drain(back_s.at[pl.ds(0, n - 1)], sends.at[RS])
-    drain(back_c.at[pl.ds(0, n - 1)], sends.at[RC])
+
+    @pl.when(central)
+    def _():
+        drain(out_c.at[pl.ds(0, n - 1)], sends.at[RC])
+
+    @pl.when(jnp.logical_not(central))
+    def _():
+        drain(out_y.at[pl.ds(0, n - 1)], sends.at[RY])
+        drain(out_z.at[pl.ds(0, n - 1)], sends.at[RZ])
 
 
 def shards(
@@ -753,7 +846,8 @@
     columns = final_weight.T
     small = (condition_flags, guidance_weights, token_frame, window_start)
     large = (video_heads, image_heads, audio_queries, audio_keys, modulation, columns)
-    if 2 * heads == n and branches == 4 and 4 * rows == 128 and rows == 2 * img_rows:
+    channels = final_weight.shape[1]
+    if 2 * heads == n and branches == 4 and 4 * rows == 128 and rows == 2 * img_rows and channels == 64:
         half = n // 2
         kernel = split_kernel
         working = [
@@ -766,16 +860,22 @@
             pltpu.VMEM((n, rows, 2 * dim), bf16),
             pltpu.VMEM((n, 1, 4 * rows), f32),
             pltpu.VMEM((n, rows, dim), bf16),
+            pltpu.VMEM((n, rows // 2, 2 * channels), bf16),
+            pltpu.VMEM((n, 1, 4 * rows), f32),
             pltpu.VMEM((n, rows, 2 * dim), bf16),
             pltpu.VMEM((n, 1, 4 * rows), f32),
-            pltpu.VMEM((n, rows, dim), bf16),
+            pltpu.VMEM((heads, rows, dim), bf16),
+            pltpu.VMEM((heads, rows // 2, 2 * channels), bf16),
+            pltpu.VMEM((heads, 1, 4 * rows), f32),
             pltpu.VMEM((plane, n // plane) + audio_keys.shape, bf16),
             pltpu.VMEM((n * audio_keys.shape[0], 2 * inner), f32),
             pltpu.VMEM((audio_queries.shape[0], rows, inner), f32),
             pltpu.VMEM((rows, inner), f32),
             pltpu.VMEM((4 * rows, 4 * rows), f32),
-            dma((8,)),
-            dma((8,)),
+            pltpu.VMEM((-(-(heads + 1) // 8) * 8, channels), f32),
+            dma((10,)),
+            dma((10,)),
+            pltpu.SemaphoreType.REGULAR,
         ]
     else:
         kernel = step_kernel

time: 58.6 us -> 56.5 us (0.964)
  Pallas kernels: 56.3 us -> 54.2 us
    pallas_call x1, Pallas kernels: 56.3 us -> 54.2 us  [shards(): pl.pallas_call(functools.partial(kernel, n, q_block, plane), out_shape=ja...]
where the time goes in v2:
time: 56.5 us; the launch traced here: 56.2 us
  Pallas kernels  54.2 us (96%)
  other arithmetic  1.35 us (2%)
  between operations  0.64 us (1%)
    pallas_call x1, Pallas kernels, shards(): pl.pallas_call(functools.partial(kernel, n, q_block, plane), out_shape=ja...  54.2 us
    sub x1, other arithmetic, shards(): return (velocity, noisy_latent - 0.125 * velocity)  1.35 us

profile of v2, /device:TPU:0, one launch (start us, length us, event | category | flops | bytes accessed | tf_op | source)
XLA Modules:
  0.0 56.2 jit_solution(6425130080105519413)
XLA Ops:
  0.6 54.2 %avatar_step.1 = f32[32,64]{1,0:T(8,128)} custom-call(s32[2,4]{1,0:T(2,128)} %flags_in.1, s32[4]{0:T(128)} %guide_in.1, s32[1024]{0:T(1024)} %frames_in.1, s32[16]{0:T(128)} %starts_in.1, bf16[16,4,32,384]{3,2,1,0:T(8,128)(2,1)} %video_in.1, bf16[16,4,16,256]{3,2,1,0:T(8,128)(2,1)} %image_in.1, bf16[2,32,2048]{2,1,0:T(8,128)(2,1)} %audio_q_in.1, ...), custom_call_target="tpu_custom_call" | custom-call | tf_op jit(solution)/shard_map/avatar_step/pallas_call | solution.py:904
  54.9 1.4 %multiply_subtract_fusion = (f32[32,64]{1,0:T(8,128)}, f32[32,64]{1,0:T(8,128)}) fusion(f32[32,64]{1,0:T(8,128)} %param.21, f32[32,64]{1,0:T(8,128)} %avatar_step.1), kind=kLoop, calls=%fused_computation | loop fusion | flops 6144 | bytes 32768 | tf_op jit(solution)/shard_map/sub | solution.py:921

commit v3 on v2

--- a/solution.py
+++ b/solution.py
@@ -673,7 +673,7 @@
         o = jnp.dot(w.astype(jnp.bfloat16), v, preferred_element_type=jnp.float32) / total
         audio_out[:, :, cols] = o.reshape(ranks, rows, dim)
 
-    loop(heads // 2, audio_head)
+    loop(3 * heads // 4, audio_head)
 
     drain(got_c.at[pl.ds(0, n - 1)], recvs.at[C])
 
@@ -725,7 +725,7 @@
         back_y[my_head] = out_y[me]
         back_z[my_head] = out_z[me]
 
-    loop(heads - heads // 2, lambda i: audio_head(heads // 2 + i))
+    loop(heads - 3 * heads // 4, lambda i: audio_head(3 * heads // 4 + i))
     swapped = jnp.where(place[0] > place[1], 1, 0)
     seats = (swapped, 1 - swapped)
 
@@ -913,7 +913,7 @@
             *working,
         ],
         compiler_params=pltpu.CompilerParams(
-            collective_id=0, has_side_effects=True, vmem_limit_bytes=67043328
+            collective_id=0, has_side_effects=True, vmem_limit_bytes=67026944
         ),
         name="avatar_step",
     )(*small, *large)

time: 56.5 us -> 55.8 us (0.988)
  Pallas kernels: 54.2 us -> 53.6 us
    pallas_call x1, Pallas kernels: 54.2 us -> 53.6 us  [shards(): pl.pallas_call(functools.partial(kernel, n, q_block, plane), out_shape=ja...]
where the time goes in v3:
time: 55.8 us; the launch traced here: 55.5 us
  Pallas kernels  53.6 us (96%)
  other arithmetic  1.33 us (2%)
  between operations  0.66 us (1%)
    pallas_call x1, Pallas kernels, shards(): pl.pallas_call(functools.partial(kernel, n, q_block, plane), out_shape=ja...  53.6 us
    sub x1, other arithmetic, shards(): return (velocity, noisy_latent - 0.125 * velocity)  1.33 us

profile of v3, /device:TPU:0, one launch (start us, length us, event | category | flops | bytes accessed | tf_op | source)
XLA Modules:
  0.0 55.5 jit_solution(16416014739334556170)
XLA Ops:
  0.6 0.0 copy-start
  0.6 53.6 %avatar_step.1 = f32[32,64]{1,0:T(8,128)} custom-call(s32[2,4]{1,0:T(2,128)} %flags_in.1, s32[4]{0:T(128)} %guide_in.1, s32[1024]{0:T(1024)} %frames_in.1, s32[16]{0:T(128)} %starts_in.1, bf16[16,4,32,384]{3,2,1,0:T(8,128)(2,1)} %video_in.1, bf16[16,4,16,256]{3,2,1,0:T(8,128)(2,1)} %image_in.1, bf16[2,32,2048]{2,1,0:T(8,128)(2,1)} %audio_q_in.1, ...), custom_call_target="tpu_custom_call" | custom-call | tf_op jit(solution)/shard_map/avatar_step/pallas_call | solution.py:904
  54.2 0.0 copy-done
  54.2 1.3 %multiply_subtract_fusion = (f32[32,64]{1,0:T(8,128)}, f32[32,64]{1,0:T(8,128)}) fusion(f32[32,64]{1,0:T(8,128)S(1)} %copy-done, f32[32,64]{1,0:T(8,128)} %avatar_step.1), kind=kLoop, calls=%fused_computation | loop fusion | flops 6144 | bytes 32768 | tf_op jit(solution)/shard_map/sub | solution.py:921
Async XLA Ops:
  0.6 53.6 %copy-start = (f32[32,64]{1,0:T(8,128)S(1)}, f32[32,64]{1,0:T(8,128)}, u32[]{:S(2)}) copy-start(f32[32,64]{1,0:T(8,128)} %param.21) | copy-start | bytes 24580

commit v4 on v3

--- a/solution.py
+++ b/solution.py
@@ -678,7 +678,7 @@
     drain(got_c.at[pl.ds(0, n - 1)], recvs.at[C])
 
     def plain_block(i):
-        b = (turn + i) % blocks
+        b = (me // per_block + i) % blocks
         devices = pl.ds(pl.multiple_of(b * per_block, per_block), per_block)
         q = got_c[devices, :, 0:dim].reshape(q_block, dim)
         k = got_c[:, :, dim : 2 * dim].reshape(n * rows, dim)

time: 55.8 us -> 55.2 us (0.989)
  Pallas kernels: 53.6 us -> 53 us
    pallas_call x1, Pallas kernels: 53.6 us -> 53 us  [shards(): pl.pallas_call(functools.partial(kernel, n, q_block, plane), out_shape=ja...]
where the time goes in v4:
time: 55.2 us; the launch traced here: 55 us
  Pallas kernels  53 us (96%)
  other arithmetic  1.33 us (2%)
  between operations  0.66 us (1%)
    pallas_call x1, Pallas kernels, shards(): pl.pallas_call(functools.partial(kernel, n, q_block, plane), out_shape=ja...  53 us
    sub x1, other arithmetic, shards(): return (velocity, noisy_latent - 0.125 * velocity)  1.33 us

profile of v4, /device:TPU:0, one launch (start us, length us, event | category | flops | bytes accessed | tf_op | source)
XLA Modules:
  0.0 55.0 jit_solution(7336333390680189963)
XLA Ops:
  0.6 0.0 copy-start
  0.6 53.0 %avatar_step.1 = f32[32,64]{1,0:T(8,128)} custom-call(s32[2,4]{1,0:T(2,128)} %flags_in.1, s32[4]{0:T(128)} %guide_in.1, s32[1024]{0:T(1024)} %frames_in.1, s32[16]{0:T(128)} %starts_in.1, bf16[16,4,32,384]{3,2,1,0:T(8,128)(2,1)} %video_in.1, bf16[16,4,16,256]{3,2,1,0:T(8,128)(2,1)} %image_in.1, bf16[2,32,2048]{2,1,0:T(8,128)(2,1)} %audio_q_in.1, ...), custom_call_target="tpu_custom_call" | custom-call | tf_op jit(solution)/shard_map/avatar_step/pallas_call | solution.py:904
  53.6 0.0 copy-done
  53.6 1.3 %multiply_subtract_fusion = (f32[32,64]{1,0:T(8,128)}, f32[32,64]{1,0:T(8,128)}) fusion(f32[32,64]{1,0:T(8,128)S(1)} %copy-done, f32[32,64]{1,0:T(8,128)} %avatar_step.1), kind=kLoop, calls=%fused_computation | loop fusion | flops 6144 | bytes 32768 | tf_op jit(solution)/shard_map/sub | solution.py:921
Async XLA Ops:
  0.6 53.0 %copy-start = (f32[32,64]{1,0:T(8,128)S(1)}, f32[32,64]{1,0:T(8,128)}, u32[]{:S(2)}) copy-start(f32[32,64]{1,0:T(8,128)} %param.21) | copy-start | bytes 24580

commit v5 on v4

--- a/solution.py
+++ b/solution.py
@@ -767,20 +767,14 @@
 
     @pl.when(central)
     def _():
-        drain(back_c.at[pl.ds(0, heads - 1)], recvs.at[RC])
         drain(back_y, recvs.at[RY])
         drain(back_z, recvs.at[RZ])
 
     @pl.when(jnp.logical_not(central))
     def _():
-        drain(back_c, recvs.at[RC])
         drain(back_y.at[pl.ds(0, heads - 1)], recvs.at[RY])
         drain(back_z.at[pl.ds(0, heads - 1)], recvs.at[RZ])
 
-    for h in range(heads):
-        cols = slice(h * dim, (h + 1) * dim)
-        hidden[:, cols] = back_c[h].astype(jnp.float32) + audio_out[seats[1], :, cols]
-    result = finish(1, result)
     z = back_z[:, 0, :]
     center = jnp.mean(z, axis=0, keepdims=True)
     away = z - center
@@ -793,6 +787,19 @@
         y = y + weights[0:rows, h : h + 1] * folded[h : h + 1, :]
     y = weights[0:rows, heads : heads + 1] * y + folded[heads : heads + 1, :]
     result = result + guide[place[3]].astype(jnp.float32) * y
+
+    @pl.when(central)
+    def _():
+        drain(back_c.at[pl.ds(0, heads - 1)], recvs.at[RC])
+
+    @pl.when(jnp.logical_not(central))
+    def _():
+        drain(back_c, recvs.at[RC])
+
+    for h in range(heads):
+        cols = slice(h * dim, (h + 1) * dim)
+        hidden[:, cols] = back_c[h].astype(jnp.float32) + audio_out[seats[1], :, cols]
+    result = finish(1, result)
     mixed[...] = result
 
     drain(gathered.at[0, pl.ds(0, strips - 1)], sends.at[FAR])

time: 55.2 us -> 55.4 us (level)
  no operation moved by 1% of the time
where the time goes in v5:
time: 55.4 us; the launch traced here: 55.1 us
  Pallas kernels  53.1 us (96%)
  other arithmetic  1.33 us (2%)
  between operations  0.66 us (1%)
    pallas_call x1, Pallas kernels, shards(): pl.pallas_call(functools.partial(kernel, n, q_block, plane), out_shape=ja...  53.1 us
    sub x1, other arithmetic, shards(): return (velocity, noisy_latent - 0.125 * velocity)  1.33 us

profile of v5, /device:TPU:0, one launch (start us, length us, event | category | flops | bytes accessed | tf_op | source)
XLA Modules:
  0.0 55.1 jit_solution(15509507550148423957)
XLA Ops:
  0.6 0.0 copy-start
  0.6 53.1 %avatar_step.1 = f32[32,64]{1,0:T(8,128)} custom-call(s32[2,4]{1,0:T(2,128)} %flags_in.1, s32[4]{0:T(128)} %guide_in.1, s32[1024]{0:T(1024)} %frames_in.1, s32[16]{0:T(128)} %starts_in.1, bf16[16,4,32,384]{3,2,1,0:T(8,128)(2,1)} %video_in.1, bf16[16,4,16,256]{3,2,1,0:T(8,128)(2,1)} %image_in.1, bf16[2,32,2048]{2,1,0:T(8,128)(2,1)} %audio_q_in.1, ...), custom_call_target="tpu_custom_call" | custom-call | tf_op jit(solution)/shard_map/avatar_step/pallas_call | solution.py:911
  53.8 0.0 copy-done
  53.8 1.3 %multiply_subtract_fusion = (f32[32,64]{1,0:T(8,128)}, f32[32,64]{1,0:T(8,128)}) fusion(f32[32,64]{1,0:T(8,128)S(1)} %copy-done, f32[32,64]{1,0:T(8,128)} %avatar_step.1), kind=kLoop, calls=%fused_computation | loop fusion | flops 6144 | bytes 32768 | tf_op jit(solution)/shard_map/sub | solution.py:928
Async XLA Ops:
  0.6 53.1 %copy-start = (f32[32,64]{1,0:T(8,128)S(1)}, f32[32,64]{1,0:T(8,128)}, u32[]{:S(2)}) copy-start(f32[32,64]{1,0:T(8,128)} %param.21) | copy-start | bytes 24580
